TPU v7x, 512 devices: a whole 4x8x8 slice. The times are simulated.
512 devices in a mesh: ep: 64 (over x, y, core), hs: 8 (over z).
Axes of the slice: x: 4, y: 8, z: 8, core: 2. Of those that a mesh axis runs over, the one named last changes fastest.
Arguments:
- tokens: bfloat16 [2048, 4096], P('ep'), may hold values from -6 to 6
- expert_ids: int32 [2048, 8], P('ep'), may hold values from 0 to 63, all different within a row; in each aligned block of 32 rows (0 to 31, 32 to 63, ...) at most 8 rows name the same one
- gate_scores: float32 [2048, 8], P('ep'), may hold values from 0.1 to 1
- gate_weight: bfloat16 [64, 4096, 1024], P('ep', None, 'hs'), may hold values from -0.09375 to 0.09375
- up_weight: bfloat16 [64, 4096, 1024], P('ep', None, 'hs'), may hold values from -0.09375 to 0.09375
- down_weight: bfloat16 [64, 1024, 4096], P('ep', 'hs'), may hold values from -0.25 to 0.25
Outputs:
- mixed: bfloat16 [2048, 4096], P('ep', 'hs')
Inputs may be any that keep to these rules, and one draw needn't show every extreme that they name: `expert_ids`: each token names 8 different experts; among the 32 tokens of one index of ep no expert is named more than 8 times, a bound that some block reaches.
All inputs are finite; a program needn't handle non-finite values.
Results may differ from a plain program's by a relative error of at most 0.015.
Values may be sent and summed in bfloat16 or wider, within the bound.
A program may use at most 64 MiB of HBM per device.

v0:
```python
import jax
import jax.numpy as jnp
from jax import lax
from jax.sharding import PartitionSpec as P


def slot_table(expert_ids, experts, capacity):
    flattened = expert_ids.reshape(-1)
    one_hot = (flattened[:, None] == jnp.arange(experts, dtype=jnp.int32)[None, :]).astype(
        jnp.int32
    )
    earlier = jnp.cumsum(one_hot, axis=0) - one_hot
    position = jnp.sum(earlier * one_hot, axis=1)
    return flattened * capacity + position


def local(tokens, expert_ids, gate_scores, gate_weight, up_weight, down_weight):
    groups = lax.axis_size("ep")
    per_token = expert_ids.shape[1]
    token_count = tokens.shape[0]
    model_width = tokens.shape[1]
    share_width = model_width // lax.axis_size("hs")
    experts = groups * gate_weight.shape[0]
    capacity = max(2, 2 * per_token * token_count // experts)
    slots = slot_table(expert_ids, experts, capacity)
    filled = (
        jnp.zeros((experts * capacity,), jnp.int32)
        .at[slots]
        .set(jnp.arange(token_count * per_token, dtype=jnp.int32) // per_token + 1)
    )
    present = (filled > 0)[:, None]
    source_row = jnp.maximum(filled - 1, 0)
    w_gate = gate_weight[0]
    w_up = up_weight[0]
    zero_value = jnp.zeros((), jnp.bfloat16)
    outgoing = jnp.where(present, tokens[source_row], zero_value).reshape(
        groups, capacity, model_width
    )
    arrived = lax.all_to_all(outgoing, "ep", split_axis=0, concat_axis=0, tiled=True)
    slot_rows = arrived.reshape(groups * capacity, model_width)
    gate_part = jnp.dot(slot_rows, w_gate, preferred_element_type=jnp.float32)
    up_part = jnp.dot(slot_rows, w_up, preferred_element_type=jnp.float32)
    hidden = (jax.nn.silu(gate_part) * up_part).astype(jnp.bfloat16)
    partial_value = jnp.dot(hidden, down_weight[0], preferred_element_type=jnp.float32)
    summed = lax.psum_scatter(
        partial_value.astype(jnp.bfloat16), "hs", scatter_dimension=1, tiled=True
    )
    returned = lax.all_to_all(
        summed.reshape(groups, capacity, share_width), "ep", split_axis=0, concat_axis=0, tiled=True
    )
    picked = returned.reshape(groups * capacity, share_width)[slots].astype(jnp.float32)
    picked = picked.reshape(token_count, per_token, share_width)
    mixed = jnp.sum(picked * gate_scores[:, :, None], axis=1)
    return mixed.astype(jnp.bfloat16)


def solution(mesh):
    placed = (
        P("ep", None),
        P("ep", None),
        P("ep", None),
        P("ep", None, "hs"),
        P("ep", None, "hs"),
        P("ep", "hs", None),
    )
    return jax.shard_map(
        local, mesh=mesh, in_specs=placed, out_specs=P("ep", "hs"), check_vma=False
    )
```

profile of v0, /device:TPU:1, one launch (start us, length us, event | category | flops | bytes accessed | tf_op | source)
XLA Modules:
  0.0 232.6 jit_solution(5383559916850542534)
XLA Ops:
  6.5 0.0 copy-start
  6.5 0.0 reduce-scatter.2.cloned.1.call-start
  6.5 0.9 copy.9
  7.4 0.1 eq.29
  7.5 0.1 eq.25
  7.6 0.7 broadcast_multiply_fusion
  8.3 0.6 reduce-window.6
  8.9 0.2 slice_reduce_fusion
  9.1 0.1 copy.8
  9.2 0.1 mul.36
  9.3 0.1 fusion.25
  9.4 1.4 scatter_custom_fusion
  10.9 0.1 broadcast_in_dim.22
  11.0 0.0 copy-done.1
  11.0 4.4 %gather_fusion = bf16[512,4096]{1,0:T(8,128)(2,1)} fusion(bf16[32,4096]{1,0:T(8,128)(2,1)S(1)} %copy-done.1, s32[1024]{0:T(1024)S(1)} %pad_clamp_fusion.1), kind=kCustom, calls=%fused_computation | custom fusion | bytes 8390656 | tf_op jit(solution)/shard_map/gather | solution.py:36
  15.3 2.5 %bitcast_select_fusion = bf16[64,8,4096]{2,1,0:T(8,128)(2,1)S(1)} fusion(bf16[512,4096]{1,0:T(8,128)(2,1)} %gather_fusion, pred[64,8]{1,0:T(8,128)(4,1)S(1)} %broadcast_in_dim.22), kind=kLoop, calls=%fused_computation.8 | loop fusion | flops 2097152 | bytes 8389120 | tf_op jit(solution)/shard_map/jit(_where)/select_n | solution.py:36
  17.9 0.0 copy-start.3
  17.9 107.7 %all_to_all.10 = bf16[64,8,4096]{2,1,0:T(8,128)(2,1)S(1)} all-to-all(bf16[64,8,4096]{2,1,0:T(8,128)(2,1)S(1)} %bitcast_select_fusion), channel_id=1, replica_groups=mesh['ep'=64,'hs'=8] {'ep'}, dimensions={0} | all-to-all | bytes 8388608 | tf_op jit(solution)/shard_map/all_to_all | solution.py:39
  125.6 2.0 copy-done.2
  127.5 0.0 copy-done.3
  127.5 1.2 fusion.2
  128.8 0.0 copy-done
  128.8 0.0 copy-done.4
  128.8 8.6 %convolution_convert_fusion = bf16[512,4096]{1,0:T(8,128)(2,1)} fusion(bf16[64,8,4096]{2,1,0:T(8,128)(2,1)} %copy-done.2, bf16[1,128,4096]{2,1,0:T(8,128)(2,1)S(1)} %copy-done, bf16[1,4096,128]{2,1,0:T(8,128)(2,1)S(1)} %copy-done.4, f32[512,128]{1,0:T(8,128)S(1)} %fusion.2), kind=kOutput, calls=%fused_computation.3 | convolution fusion | flops 1076232192 | bytes 10747904 | tf_op jit(solution)/shard_map/dot_general | solution.py:44
  137.4 0.0 reduce-scatter.2.cloned.1.call-update
  137.4 58.5 %reduce-scatter.2.cloned.1.call-done = bf16[512,512]{1,0:T(8,128)(2,1)} async-done(((bf16[512,4096]{1,0:T(8,128)(2,1)}), bf16[512,512]{1,0:T(8,128)(2,1)}) %reduce-scatter.2.cloned.1.call-update) | async-done | bytes 524304 | tf_op jit(solution)/shard_map/reduce_scatter | solution.py:45
  196.0 10.4 %all-to-all-start.1 = ((bf16[64,8,512]{2,1,0:T(8,128)(2,1)}), bf16[64,8,512]{2,1,0:T(8,128)(2,1)S(1)}, u32[]{:S(2)}, u32[]{:S(2)}) async-start(bf16[64,8,512]{2,1,0:T(8,128)(2,1)} %bitcast.50), calls=%async_computation.2 | async-start | bytes 1048576 | tf_op jit(solution)/shard_map/all_to_all | solution.py:48
  206.4 0.0 copy-done.5
  206.4 0.1 copy.12
  206.5 17.2 %all-to-all-done.1 = bf16[64,8,512]{2,1,0:T(8,128)(2,1)S(1)} async-done(((bf16[64,8,512]{2,1,0:T(8,128)(2,1)}), bf16[64,8,512]{2,1,0:T(8,128)(2,1)S(1)}, u32[]{:S(2)}, u32[]{:S(2)}) %all-to-all-start.1) | async-done | bytes 524320 | tf_op jit(solution)/shard_map/all_to_all | solution.py:48
  223.7 1.2 gather_fusion.1
  224.9 0.8 fusion.16
  (13 shorter events, 0.1 us)
Async XLA Ops:
  6.5 122.3 %copy-start = (bf16[1,128,4096]{2,1,0:T(8,128)(2,1)S(1)}, bf16[1,128,4096]{2,1,0:T(8,128)(2,1)}, u32[]{:S(2)}) copy-start(bf16[1,128,4096]{2,1,0:T(8,128)(2,1)} %param.11) | copy-start | bytes 3145732
  6.5 4.4 %copy-start.1 = (bf16[32,4096]{1,0:T(8,128)(2,1)S(1)}, bf16[32,4096]{1,0:T(8,128)(2,1)}, u32[]{:S(2)}) copy-start(bf16[32,4096]{1,0:T(8,128)(2,1)} %param.6) | copy-start | bytes 786436
  6.5 189.4 %reduce-scatter.2.cloned.1.call-start = ((), (), s32[]{:S(2)}) async-start(), calls=%async_computation.3 | async-start | bytes 4718592 | tf_op jit(solution)/shard_map/reduce_scatter | solution.py:45
  17.9 109.7 %copy-start.3 = (bf16[1,4096,128]{2,1,0:T(8,128)(2,1)S(1)}, bf16[1,4096,128]{2,1,0:T(8,128)(2,1)}, u32[]{:S(2)}) copy-start(bf16[1,4096,128]{2,1,0:T(8,128)(2,1)} %param.9) | copy-start | bytes 3145732
  125.6 2.0 copy-start.2
  127.5 1.3 copy-start.4
  137.4 69.0 %copy-start.5 = (f32[32,8]{0,1:T(8,128)S(1)}, f32[32,8]{0,1:T(8,128)}, u32[]{:S(2)}) copy-start(f32[32,8]{0,1:T(8,128)} %param.8) | copy-start | bytes 3076
  196.0 27.7 %all-to-all-start.1 = ((bf16[64,8,512]{2,1,0:T(8,128)(2,1)}), bf16[64,8,512]{2,1,0:T(8,128)(2,1)S(1)}, u32[]{:S(2)}, u32[]{:S(2)}) async-start(bf16[64,8,512]{2,1,0:T(8,128)(2,1)} %bitcast.50), calls=%async_computation.2 | async-start | bytes 1048576 | tf_op jit(solution)/shard_map/all_to_all | solution.py:48
Sparse Core Ops, SparseCore 0:
  137.5 58.3 reduce-scatter.1
where the time goes:
time: 233 us
  blocking collectives  108 us (46%)
  waiting for transfers between devices  75.8 us (33%)
  between operations  13.5 us (6%)
  local copies, waits for them, and re-layouts  10.5 us (5%)
  starting transfers between devices  10.5 us (5%)
  matrix products  9.84 us (4%)
  other arithmetic  4.86 us (2%)
    all_to_all x1, blocking collectives, local(): lax.all_to_all(outgoing, 'ep', split_axis=0, concat_axis=0, tiled=True)  108 us
    reduce_scatter x1, waiting for transfers between devices, local(): lax.psum_scatter(partial_value.astype(jnp.bfloat16), 'hs', scatter_dimens...  58.5 us
    all_to_all x1, waiting for transfers between devices, local(): lax.all_to_all(summed.reshape(groups, capacity, share_width), 'ep', split...  17.2 us
    all_to_all x1, starting transfers between devices, local(): lax.all_to_all(summed.reshape(groups, capacity, share_width), 'ep', split...  10.4 us
    dot_general x1, matrix products, local(): jnp.dot(hidden, down_weight[0], preferred_element_type=jnp.float32)  8.59 us
  transfers between devices with their start and end apart: 2, of which 2 were waited for; matrix products, arithmetic and copies ran while one was open for 0% of the time, Pallas kernels for 0%

commit v1 on v0

v1 whole, which is shorter than its diff:
```python
import functools

import jax
import jax.numpy as jnp
from jax import lax
from jax.experimental import pallas as pl
from jax.experimental.pallas import tpu as pltpu
from jax.sharding import PartitionSpec as P

MESH = pl.DeviceIdType.MESH
F32, BF16 = jnp.float32, jnp.bfloat16


def dot(a, b):
    return jnp.dot(a, b, preferred_element_type=F32)


def iota(shape, dim):
    return lax.broadcasted_iota(jnp.int32, shape, dim)


def kernel(ne, nh, cap, parts,
           tok_hbm, ids_ref, score_ref, wg_hbm, wu_hbm, wd_hbm, out_ref,
           tok_v, xs, xb, wgu, wdt, acc, hb, ys, yb, yacc,
           local_sem, self_sem, xs_send, xs_recv, wd_send, wd_recv,
           ring_send, ring_recv, hid_send, hid_recv, y_send, y_recv):
    me = lax.axis_index("ep")
    z = lax.axis_index("hs")
    tokens, top = ids_ref.shape
    width = tok_v.shape[-1]
    units = wd_hbm.shape[1]
    half = nh // 2
    rows = ne * cap
    up_z, down_z = lax.rem(z + 1, nh), lax.rem(z + nh - 1, nh)
    far = lax.rem(z + half, nh)

    def plane(step):
        return lax.rem(z + step + nh, nh)

    barrier = pltpu.get_barrier_semaphore()

    def greet_ep(j, c):
        pl.semaphore_signal(barrier, inc=1, device_id={"ep": lax.rem(me + j, ne)}, device_id_type=MESH)
        return c

    def greet_hs(j, c):
        pl.semaphore_signal(barrier, inc=1, device_id={"hs": lax.rem(z + j, nh)}, device_id_type=MESH)
        return c

    lax.fori_loop(1, ne, greet_ep, 0)
    lax.fori_loop(1, nh, greet_hs, 0)

    def columns(s):
        return pl.ds(pl.multiple_of(s * width, width), width)

    loads = [
        pltpu.make_async_copy(tok_hbm.at[:, columns(z)], tok_v.at[0], local_sem.at[0]),
        pltpu.make_async_copy(tok_hbm.at[:, columns(far)], tok_v.at[1], local_sem.at[1]),
        pltpu.make_async_copy(wg_hbm.at[0], wgu.at[:, pl.ds(0, units)], local_sem.at[2]),
        pltpu.make_async_copy(wu_hbm.at[0], wgu.at[:, pl.ds(units, units)], local_sem.at[3]),
        pltpu.make_async_copy(wd_hbm.at[0, :, columns(z)], wdt.at[z], local_sem.at[4]),
    ]
    for load in loads:
        load.start()

    ids = ids_ref[...]
    gates = score_ref[...]
    named = jnp.zeros((tokens, ne), F32)
    score = jnp.zeros((tokens, ne), F32)
    lane = iota((tokens, ne), 1)
    for k in range(top):
        hit = ids[:, k:k + 1] == lane
        named = named + jnp.where(hit, 1.0, 0.0)
        score = score + jnp.where(hit, gates[:, k:k + 1], 0.0)
    before = jnp.where(iota((tokens, tokens), 1) < iota((tokens, tokens), 0), 1.0, 0.0).astype(BF16)
    place = dot(before, named.astype(BF16))
    mark = (named * (place + 1.0)).astype(BF16)
    spread = jnp.where(iota((rows, ne), 0) // cap == iota((rows, ne), 1), 1.0, 0.0).astype(BF16)
    nt = (((1,), (1,)), ((), ()))
    mark_rows = lax.dot_general(spread, mark, nt, preferred_element_type=F32)
    slot_row = (iota((rows, tokens), 0) % cap + 1).astype(F32)
    pick = jnp.where(mark_rows == slot_row, 1.0, 0.0).astype(BF16)

    loads[0].wait()
    xs[0] = dot(pick, tok_v[0]).reshape(ne, cap, width).astype(BF16)
    loads[1].wait()
    xs[1] = dot(pick, tok_v[1]).reshape(ne, cap, width).astype(BF16)

    mark_cols = lax.dot_general(mark, spread, nt, preferred_element_type=F32)
    slot_col = (iota((tokens, rows), 1) % cap + 1).astype(F32)
    score_high = score.astype(BF16)
    score_low = (score - score_high.astype(F32)).astype(BF16)
    here = mark_cols == slot_col
    gate_high = jnp.where(
        here, lax.dot_general(score_high, spread, nt, preferred_element_type=F32), 0.0).astype(BF16)
    gate_low = jnp.where(
        here, lax.dot_general(score_low, spread, nt, preferred_element_type=F32), 0.0).astype(BF16)

    pl.semaphore_wait(barrier, ne - 1 + nh - 1)

    def send_rows(q, s):
        def body(j, c):
            dest = lax.rem(me + j * 27, ne)
            pltpu.make_async_remote_copy(
                src_ref=xs.at[q, dest], dst_ref=xb.at[s, me],
                send_sem=xs_send.at[q], recv_sem=xs_recv.at[q],
                device_id={"ep": dest}, device_id_type=MESH).start()
            return c
        lax.fori_loop(1, ne, body, 0)

    send_rows(0, z)
    self_copies = [
        pltpu.make_async_copy(xs.at[0, me], xb.at[z, me], self_sem.at[0]),
        pltpu.make_async_copy(xs.at[1, me], xb.at[far, me], self_sem.at[1]),
    ]
    for copy in self_copies:
        copy.start()

    def send_down(j, c):
        dest = lax.rem(z + j, nh)
        pltpu.make_async_remote_copy(
            src_ref=wd_hbm.at[0, :, columns(dest)], dst_ref=wdt.at[z],
            send_sem=wd_send, recv_sem=wd_recv,
            device_id={"hs": dest}, device_id_type=MESH).start()
        return c

    lax.fori_loop(1, nh, send_down, 0)
    send_rows(1, far)

    def all_but_own(ref, sem):
        view = ref.at[pl.ds(0, ref.shape[0] - 1)]
        return pltpu.make_async_copy(view, view, sem)

    group = ne // parts
    chunk = group * cap

    def ring(direction, step, part):
        s = plane(-step) if direction == 0 else plane(step)
        view = xb.at[s, pl.ds(part * group, group)]
        return pltpu.make_async_remote_copy(
            src_ref=view, dst_ref=view,
            send_sem=ring_send.at[direction, step, part], recv_sem=ring_recv.at[direction, step, part],
            device_id={"hs": up_z if direction == 0 else down_z}, device_id_type=MESH)

    def arrived(direction, step, part):
        s = plane(-1 - step) if direction == 0 else plane(1 + step)
        view = xb.at[s, pl.ds(part * group, group)]
        return s, pltpu.make_async_copy(view, view, ring_recv.at[direction, step, part])

    def weights(s):
        return wgu[pl.ds(pl.multiple_of(s * width, width), width), :]

    def rows_of(s, part):
        return xb[s, pl.ds(part * group, group)].reshape(chunk, width)

    self_copies[0].wait()
    all_but_own(xb.at[z], xs_recv.at[0]).wait()

    steps = half - 1

    def start_ring(part, c):
        ring(0, 0, part).start()
        ring(1, 0, part).start()
        return c

    lax.fori_loop(0, parts, start_ring, 0)
    loads[2].wait()
    loads[3].wait()

    def first(part, c):
        acc[pl.ds(part * chunk, chunk), :] = dot(rows_of(z, part), weights(z))
        return c

    lax.fori_loop(0, parts, first, 0)

    for step in range(steps):
        def body(part, c, step=step):
            s_up, got_up = arrived(0, step, part)
            got_up.wait()
            if step + 1 < steps:
                ring(0, step + 1, part).start()
            s_down, got_down = arrived(1, step, part)
            got_down.wait()
            if step + 1 < steps:
                ring(1, step + 1, part).start()
            acc[pl.ds(part * chunk, chunk), :] += (
                dot(rows_of(s_up, part), weights(s_up)) + dot(rows_of(s_down, part), weights(s_down)))
            return c
        lax.fori_loop(0, parts, body, 0)
        if step == 0:
            self_copies[1].wait()
            all_but_own(xb.at[far], xs_recv.at[1]).wait()

            def second(part, c):
                acc[pl.ds(part * chunk, chunk), :] += dot(rows_of(far, part), weights(far))
                return c

            lax.fori_loop(0, parts, second, 0)

    hrows = rows // 2

    def hid(direction, step, part):
        s = plane(-step) if direction == 0 else plane(step)
        view = hb.at[s, pl.ds(part * hrows, hrows)]
        return pltpu.make_async_remote_copy(
            src_ref=view, dst_ref=view,
            send_sem=hid_send.at[direction, step, part], recv_sem=hid_recv.at[direction, step, part],
            device_id={"hs": up_z if direction == 0 else down_z}, device_id_type=MESH)

    def hid_arrived(direction, step, part):
        s = plane(-1 - step) if direction == 0 else plane(1 + step)
        view = hb.at[s, pl.ds(part * hrows, hrows)]
        return s, pltpu.make_async_copy(view, view, hid_recv.at[direction, step, part])

    for part in range(2):
        gate = acc[part * hrows:(part + 1) * hrows, 0:units]
        upper = acc[part * hrows:(part + 1) * hrows, units:2 * units]
        hb[z, part * hrows:(part + 1) * hrows, :] = (
            gate / (1.0 + jnp.exp(-gate)) * upper).astype(BF16)
        hid(0, 0, part).start()
        hid(1, 0, part).start()

    loads[4].wait()
    all_but_own(wdt, wd_recv).wait()

    def out_part(s, part):
        return dot(hb[s, part * hrows:(part + 1) * hrows, :], wdt[s])

    for part in range(2):
        yacc[part * hrows:(part + 1) * hrows, :] = out_part(z, part)
    for step in range(steps):
        for part in range(2):
            s_up, got_up = hid_arrived(0, step, part)
            s_down, got_down = hid_arrived(1, step, part)
            got_up.wait()
            if step + 1 < steps or part == 0:
                hid(0, step + 1, part).start()
            got_down.wait()
            if step + 1 < steps or part == 1:
                hid(1, step + 1, part).start()
            yacc[part * hrows:(part + 1) * hrows, :] += out_part(s_up, part) + out_part(s_down, part)

    half_blocks = ne // 2
    for part in range(2):
        _, got = hid_arrived(part, steps, part)
        got.wait()
        total = yacc[part * hrows:(part + 1) * hrows, :] + out_part(far, part)
        ys[part * half_blocks:(part + 1) * half_blocks] = (
            total.reshape(half_blocks, cap, width).astype(BF16))

        def send_back(j, c, part=part):
            dest = part * half_blocks + lax.rem(me + j * 11, half_blocks)

            @pl.when(dest != me)
            def _():
                pltpu.make_async_remote_copy(
                    src_ref=ys.at[dest], dst_ref=yb.at[me],
                    send_sem=y_send, recv_sem=y_recv,
                    device_id={"ep": dest}, device_id_type=MESH).start()
            return c

        lax.fori_loop(0, half_blocks, send_back, 0)

    own = pltpu.make_async_copy(ys.at[me], yb.at[me], self_sem.at[2])
    own.start()
    own.wait()
    all_but_own(yb, y_recv).wait()
    back = yb[...].reshape(rows, width)
    out_ref[...] = (dot(gate_high, back) + dot(gate_low, back)).astype(BF16)

    for q in range(2):
        all_but_own(xs.at[q], xs_send.at[q]).wait()
    all_but_own(wdt, wd_send).wait()
    all_but_own(ys, y_send).wait()

    def drain(part, c):
        for direction in range(2):
            for step in range(steps):
                ring(direction, step, part).wait_send()
        return c

    lax.fori_loop(0, parts, drain, 0)
    for direction in range(2):
        for part in range(2):
            for step in range(steps):
                hid(direction, step, part).wait_send()
        hid(direction, steps, direction).wait_send()


def local(tokens, expert_ids, gate_scores, gate_weight, up_weight, down_weight):
    ne, nh = lax.axis_size("ep"), lax.axis_size("hs")
    count, model = tokens.shape
    width = model // nh
    units = gate_weight.shape[2]
    cap = max(2, 2 * expert_ids.shape[1] * count // ne)
    rows = ne * cap
    parts = 4
    steps = nh // 2 - 1
    dma = pltpu.SemaphoreType.DMA
    anywhere = pl.BlockSpec(memory_space=pl.ANY)
    vmem = pl.BlockSpec(memory_space=pltpu.VMEM)
    return pl.pallas_call(
        functools.partial(kernel, ne, nh, cap, parts),
        out_shape=jax.ShapeDtypeStruct((count, width), BF16),
        in_specs=[anywhere, vmem, vmem, anywhere, anywhere, anywhere],
        out_specs=vmem,
        scratch_shapes=[
            pltpu.VMEM((2, count, width), BF16),
            pltpu.VMEM((2, ne, cap, width), BF16),
            pltpu.VMEM((nh, ne, cap, width), BF16),
            pltpu.VMEM((model, 2 * units), BF16),
            pltpu.VMEM((nh, units, width), BF16),
            pltpu.VMEM((rows, 2 * units), F32),
            pltpu.VMEM((nh, rows, units), BF16),
            pltpu.VMEM((ne, cap, width), BF16),
            pltpu.VMEM((ne, cap, width), BF16),
            pltpu.VMEM((rows, width), F32),
            dma((5,)), dma((3,)), dma((2,)), dma((2,)), dma, dma,
            dma((2, steps, parts)), dma((2, steps, parts)),
            dma((2, steps + 1, 2)), dma((2, steps + 1, 2)), dma, dma,
        ],
        compiler_params=pltpu.CompilerParams(
            collective_id=0, has_side_effects=True, vmem_limit_bytes=48 << 20),
    )(tokens, expert_ids, gate_scores, gate_weight, up_weight, down_weight)


def solution(mesh):
    placed = (
        P("ep", None),
        P("ep", None),
        P("ep", None),
        P("ep", None, "hs"),
        P("ep", None, "hs"),
        P("ep", "hs", None),
    )
    return jax.shard_map(
        local, mesh=mesh, in_specs=placed, out_specs=P("ep", "hs"), check_vma=False
    )
```

time: 233 us -> 108 us (0.46)
  blocking collectives: 108 us -> 0 us
  Pallas kernels: 0 us -> 101 us
  waiting for transfers between devices: 75.8 us -> 0 us
  between operations: 13.5 us -> 0.02 us
  starting transfers between devices: 10.5 us -> 0 us
  matrix products: 9.84 us -> 0 us
  other arithmetic: 4.86 us -> 0 us
  local copies, waits for them, and re-layouts: 10.5 us -> 6.09 us
    all_to_all x1 -> x0, blocking collectives: 108 us -> none  [local(): lax.all_to_all(outgoing, 'ep', split_axis=0, concat_axis=0, tiled=True)]
    pallas_call x0 -> x1, Pallas kernels: none -> 101 us  [local(): pl.pallas_call(functools.partial(kernel, ne, nh, cap, parts), out_shape=j...]
    reduce_scatter x1 -> x0, waiting for transfers between devices: 58.5 us -> none  [local(): lax.psum_scatter(partial_value.astype(jnp.bfloat16), 'hs', scatter_dimens...]
    all_to_all x1 -> x0, waiting for transfers between devices: 17.2 us -> none  [local(): lax.all_to_all(summed.reshape(groups, capacity, share_width), 'ep', split...]
    all_to_all x1 -> x0, starting transfers between devices: 10.4 us -> none  [local(): lax.all_to_all(summed.reshape(groups, capacity, share_width), 'ep', split...]
    dot_general x2 -> x0, matrix products: 9.84 us -> none  [the longest x1 8.59 us: local(): jnp.dot(hidden, down_weight[0], preferred_element_type=jnp.float32)]
    gather x2 -> x0, local copies, waits for them, and re-layouts: 5.5 us -> none  [the longest x1 4.35 us: local(): tokens[source_row]]
    unnamed x14 -> x13, local copies, waits for them, and re-layouts: 2.93 us -> 6.09 us
  transfers between devices with their start and end apart: 2 -> 0, of which waited for: 2 -> 0; matrix products, arithmetic and copies ran while one was open for 0% -> 0% of each run, Pallas kernels for 0% -> 0%
where the time goes in v1:
time: 108 us; the launch traced here: 107 us
  Pallas kernels  101 us (94%)
  local copies, waits for them, and re-layouts  6.09 us (6%)
    pallas_call x1, Pallas kernels, local(): pl.pallas_call(functools.partial(kernel, ne, nh, cap, parts), out_shape=j...  101 us
    unnamed x13, local copies, waits for them, and re-layouts  6.09 us

profile of v1, /device:TPU:1, one launch (start us, length us, event | category | flops | bytes accessed | tf_op | source)
XLA Modules:
  0.0 106.8 jit_solution(3878110818048453169)
XLA Ops:
  0.0 0.0 copy-start.4
  0.0 0.8 copy.7.ids_ref
  0.8 0.0 copy-done.4
  0.8 0.1 copy.8.score_ref
  0.9 0.0 copy-start
  0.9 1.2 %copy-done = bf16[1,4096,128]{2,1,0:T(8,128)(2,1)S(1)} copy-done((bf16[1,4096,128]{2,1,0:T(8,128)(2,1)S(1)}, bf16[1,4096,128]{2,1,0:T(8,128)(2,1)}, u32[]{:S(2)}) %copy-start) | copy-done | bytes 1048600
  2.1 0.0 copy-start.1
  2.1 1.2 %copy-done.1 = bf16[1,4096,128]{2,1,0:T(8,128)(2,1)S(1)} copy-done((bf16[1,4096,128]{2,1,0:T(8,128)(2,1)S(1)}, bf16[1,4096,128]{2,1,0:T(8,128)(2,1)}, u32[]{:S(2)}) %copy-start.1) | copy-done | bytes 1048600
  3.3 0.0 copy-start.2
  3.3 1.2 %copy-done.2 = bf16[1,128,4096]{2,1,0:T(8,128)(2,1)S(1)} copy-done((bf16[1,128,4096]{2,1,0:T(8,128)(2,1)S(1)}, bf16[1,128,4096]{2,1,0:T(8,128)(2,1)}, u32[]{:S(2)}) %copy-start.2) | copy-done | bytes 1048600
  4.5 0.0 copy-start.3
  4.5 0.9 copy-done.3
  5.5 100.7 %shard_map.64 = bf16[32,512]{1,0:T(8,128)(2,1)S(1)} custom-call(bf16[32,4096]{1,0:T(8,128)(2,1)S(1)} %copy-done.3, s32[32,8]{1,0:T(8,128)S(1)} %copy.7.ids_ref, f32[32,8]{1,0:T(8,128)S(1)} %copy.8.score_ref, bf16[1,4096,128]{2,1,0:T(8,128)(2,1)S(1)} %copy-done, bf16[1,4096,128]{2,1,0:T(8,128)(2,1)S(1)} %copy-done.1, bf16[1,128,4096]{2,1,0:T(8,128)(2,1)S(1)} %copy-done.2), custom_call_target="tpu_custom_call" | custom-call | tf_op jit(solution)/shard_map/pallas_call | solution.py:302
  106.2 0.6 copy.10
Async XLA Ops:
  0.0 0.8 copy-start.4
  0.9 1.2 %copy-start = (bf16[1,4096,128]{2,1,0:T(8,128)(2,1)S(1)}, bf16[1,4096,128]{2,1,0:T(8,128)(2,1)}, u32[]{:S(2)}) copy-start(bf16[1,4096,128]{2,1,0:T(8,128)(2,1)} %wg_hbm.1) | copy-start | bytes 3145732
  2.1 1.2 %copy-start.1 = (bf16[1,4096,128]{2,1,0:T(8,128)(2,1)S(1)}, bf16[1,4096,128]{2,1,0:T(8,128)(2,1)}, u32[]{:S(2)}) copy-start(bf16[1,4096,128]{2,1,0:T(8,128)(2,1)} %wu_hbm.1) | copy-start | bytes 3145732
  3.3 1.2 %copy-start.2 = (bf16[1,128,4096]{2,1,0:T(8,128)(2,1)S(1)}, bf16[1,128,4096]{2,1,0:T(8,128)(2,1)}, u32[]{:S(2)}) copy-start(bf16[1,128,4096]{2,1,0:T(8,128)(2,1)} %wd_hbm.1) | copy-start | bytes 3145732
  4.5 0.9 copy-start.3

commit v2 on v1

v2 whole, which is shorter than its diff:
```python
import functools

import jax
import jax.numpy as jnp
from jax import lax
from jax.experimental import pallas as pl
from jax.experimental.pallas import tpu as pltpu
from jax.sharding import PartitionSpec as P

MESH = pl.DeviceIdType.MESH
F32, BF16 = jnp.float32, jnp.bfloat16
CHIPS_Y, CORES = 8, 2


def dot(a, b):
    return jnp.dot(a, b, preferred_element_type=F32)


def dot_nt(a, b):
    return lax.dot_general(a, b, (((1,), (1,)), ((), ())), preferred_element_type=F32)


def iota(shape, dim):
    return lax.broadcasted_iota(jnp.int32, shape, dim)


def ones_where(condition):
    return jnp.where(condition, 1.0, 0.0).astype(BF16)


def kernel(ne, nh, ny, cap, slices,
           tok_hbm, ids_ref, score_ref, wg_hbm, wu_hbm, wd_hbm, out_ref,
           tok_v, mk, mb, tb, pick, xs, xb, wgu, wdt, acc, hb, ys, yb, yacc,
           load_sem, own_sem, self_sem, mk_send, mk_recv, tok_send, tok_recv, x_send, x_recv,
           wd_send, wd_recv, ring_send, ring_recv, hid_send, hid_recv, y_send, y_recv):
    me = lax.axis_index("ep")
    z = lax.axis_index("hs")
    nc = CORES
    nx = ne // (ny * nc)
    c = lax.rem(me, nc)
    y = lax.rem(me // nc, ny)
    x = me // (nc * ny)
    top, tokens = ids_ref.shape
    width = yacc.shape[-1]
    part_width = width // nc
    units = wd_hbm.shape[1]
    half = nh // 2
    rows = ne * cap
    nq = ny * nc
    nd = nx * nc
    q = lax.rem(me, nq)
    d = x * nc + c
    count = len(slices)
    up_z, down_z = lax.rem(z + 1, nh), lax.rem(z + nh - 1, nh)
    far = lax.rem(z + half, nh)

    def plane(step):
        return lax.rem(z + step + nh, nh)

    barrier = pltpu.get_barrier_semaphore()

    def greet_ep(j, carry):
        pl.semaphore_signal(barrier, inc=1, device_id={"ep": lax.rem(me + j, ne)}, device_id_type=MESH)
        return carry

    def greet_hs(j, carry):
        pl.semaphore_signal(barrier, inc=1, device_id={"hs": lax.rem(z + j, nh)}, device_id_type=MESH)
        return carry

    lax.fori_loop(1, ne, greet_ep, 0)
    lax.fori_loop(1, nh, greet_hs, 0)

    def columns(s):
        return pl.ds(pl.multiple_of(s * width, width), width)

    def part_columns(s, part):
        return pl.ds(pl.multiple_of(s * width + part * part_width, part_width), part_width)

    loads = [
        pltpu.make_async_copy(tok_hbm, tok_v, load_sem.at[0]),
        pltpu.make_async_copy(wg_hbm.at[0], wgu.at[:, pl.ds(0, units)], load_sem.at[1]),
        pltpu.make_async_copy(wu_hbm.at[0], wgu.at[:, pl.ds(units, units)], load_sem.at[2]),
        pltpu.make_async_copy(wd_hbm.at[0, :, columns(z)], wdt.at[z], load_sem.at[3]),
    ]
    own_tokens = [
        pltpu.make_async_copy(tok_hbm.at[:, part_columns(plane(rel), c)], tb.at[r, q], own_sem.at[r])
        for r, rel in enumerate(slices)
    ]
    for load in loads[:1] + own_tokens + loads[1:]:
        load.start()

    ids = ids_ref[...]
    gates = score_ref[...]
    order = iota((ne, tokens), 0)
    expert = (lax.rem(order, nd) // nc * ny + order // nd) * nc + lax.rem(order, nc)
    named = jnp.zeros((ne, tokens), F32)
    score = jnp.zeros((ne, tokens), F32)
    for k in range(top):
        hit = ids[k:k + 1, :] == expert
        named = named + jnp.where(hit, 1.0, 0.0)
        score = score + jnp.where(hit, gates[k:k + 1, :], 0.0)
    before = ones_where(iota((tokens, tokens), 0) < iota((tokens, tokens), 1))
    mark = (named * (dot(named.astype(BF16), before) + 1.0)).astype(BF16)
    per_group = 128 // tokens
    shift = ones_where(
        iota((tokens, 128), 1) == iota((tokens, 128), 0) + lax.rem(q, per_group) * tokens)
    mk[...] = dot(mark, shift).reshape(ny, nd, 128)

    loads[0].wait()
    pl.semaphore_wait(barrier, ne - 1 + nh - 1)

    def along_y(j):
        other = lax.rem(q + j, nq)
        return other, {"ep": x * nq + other}

    def send_tokens(r, rel):
        def body(j, carry):
            other, device = along_y(j)
            pltpu.make_async_remote_copy(
                src_ref=tok_v.at[:, part_columns(plane(rel), lax.rem(other, nc))], dst_ref=tb.at[r, q],
                send_sem=tok_send.at[r], recv_sem=tok_recv.at[r],
                device_id=device, device_id_type=MESH).start()
            return carry
        lax.fori_loop(1, nq, body, 0)

    def send_marks(j, carry):
        other, device = along_y(j)
        pltpu.make_async_remote_copy(
            src_ref=mk.at[other // nc], dst_ref=mb.at[q], send_sem=mk_send, recv_sem=mk_recv,
            device_id=device, device_id_type=MESH).start()
        return carry

    lax.fori_loop(1, nq, send_marks, 0)
    own_marks = pltpu.make_async_copy(mk.at[y], mb.at[q], self_sem.at[0])
    own_marks.start()
    send_tokens(0, slices[0])

    def send_down(j, carry):
        dest = lax.rem(z + j, nh)
        pltpu.make_async_remote_copy(
            src_ref=wd_hbm.at[0, :, columns(dest)], dst_ref=wdt.at[z],
            send_sem=wd_send, recv_sem=wd_recv,
            device_id={"hs": dest}, device_id_type=MESH).start()
        return carry

    lax.fori_loop(1, nh, send_down, 0)
    for r in range(1, count):
        send_tokens(r, slices[r])

    spread = ones_where(iota((rows, ne), 0) // cap == iota((rows, ne), 1))
    here = dot(spread, mark) == (lax.rem(iota((rows, tokens), 0), cap) + 1).astype(F32)
    score_high = score.astype(BF16)
    score_low = (score - score_high.astype(F32)).astype(BF16)
    same = ones_where(iota((tokens, tokens), 0) == iota((tokens, tokens), 1))
    gate_high = dot_nt(same, jnp.where(here, dot(spread, score_high), 0.0).astype(BF16)).astype(BF16)
    gate_low = dot_nt(same, jnp.where(here, dot(spread, score_low), 0.0).astype(BF16)).astype(BF16)

    def bytes_of(view, sem):
        return pltpu.make_async_copy(view, view, sem)

    own_marks.wait()
    bytes_of(mb.at[pl.ds(0, nq - 1)], mk_recv).wait()
    marks = jnp.concatenate(
        [sum(mb[g * per_group + i] for i in range(per_group)) for g in range(nq // per_group)], axis=1)
    q_rows, q_lanes = nq * cap, nq * tokens
    slot = (lax.rem(iota((q_rows, q_lanes), 0), cap) + 1).astype(F32)
    slot = jnp.where(iota((q_rows, q_lanes), 0) // cap == iota((q_rows, q_lanes), 1) // tokens, slot, -1.0)
    for i in range(nd):
        pick[i] = ones_where(marks[i:i + 1, :] == slot)

    def select(r):
        own_tokens[r].wait()
        bytes_of(tb.at[r, pl.ds(0, nq - 1)], tok_recv.at[r]).wait()
        block = tb[r].reshape(q_lanes, part_width)
        s = plane(slices[r])

        def body(j, carry):
            i = lax.rem(d + j, nd)
            xs[r, i] = dot(pick[i], block).astype(BF16)
            pltpu.make_async_remote_copy(
                src_ref=xs.at[r, i],
                dst_ref=xb.at[s, x, :, pl.ds(pl.multiple_of(c * part_width, part_width), part_width)],
                send_sem=x_send.at[r], recv_sem=x_recv.at[r],
                device_id={"ep": (i // nc * ny + y) * nc + lax.rem(i, nc)}, device_id_type=MESH).start()
            return carry

        lax.fori_loop(1, nd, body, 0)
        xb[s, x, :, pl.ds(pl.multiple_of(c * part_width, part_width), part_width)] = (
            dot(pick[d], block).astype(BF16))

    def weights(s):
        return wgu[pl.ds(pl.multiple_of(s * width, width), width), :]

    def multiply(s, first=False):
        product = dot(xb[s].reshape(rows, width), weights(s))
        if first:
            acc[...] = product
        else:
            acc[...] += product

    def ring(direction, part):
        view = xb.at[z, part]
        return pltpu.make_async_remote_copy(
            src_ref=view, dst_ref=view,
            send_sem=ring_send.at[direction, part], recv_sem=ring_recv.at[direction, part],
            device_id={"hs": up_z if direction == 0 else down_z}, device_id_type=MESH)

    def collect(r):
        bytes_of(xs.at[r, pl.ds(0, nd - 1)], x_recv.at[r]).wait()
        if r == 0:
            for part in range(nx):
                ring(0, part).start()
                ring(1, part).start()
            loads[1].wait()
            loads[2].wait()
        multiply(plane(slices[r]), first=r == 0)

    select(0)
    for r in range(1, count):
        select(r)
        collect(r - 1)

    for direction, s in ((0, plane(-1)), (1, plane(1))):
        for part in range(nx):
            view = xb.at[s, part]
            bytes_of(view, ring_recv.at[direction, part]).wait()
        multiply(s)
    collect(count - 1)

    steps = half - 1
    hrows = rows // 2

    def hid(direction, step, part):
        s = plane(-step) if direction == 0 else plane(step)
        view = hb.at[s, pl.ds(part * hrows, hrows)]
        return pltpu.make_async_remote_copy(
            src_ref=view, dst_ref=view,
            send_sem=hid_send.at[direction, step, part], recv_sem=hid_recv.at[direction, step, part],
            device_id={"hs": up_z if direction == 0 else down_z}, device_id_type=MESH)

    def hid_arrived(direction, step, part):
        s = plane(-1 - step) if direction == 0 else plane(1 + step)
        view = hb.at[s, pl.ds(part * hrows, hrows)]
        return s, bytes_of(view, hid_recv.at[direction, step, part])

    for part in range(2):
        gate = acc[part * hrows:(part + 1) * hrows, 0:units]
        upper = acc[part * hrows:(part + 1) * hrows, units:2 * units]
        hb[z, part * hrows:(part + 1) * hrows, :] = (
            gate / (1.0 + jnp.exp(-gate)) * upper).astype(BF16)
        hid(0, 0, part).start()
        hid(1, 0, part).start()

    loads[3].wait()
    bytes_of(wdt.at[pl.ds(0, nh - 1)], wd_recv).wait()

    def out_part(s, part):
        return dot(hb[s, part * hrows:(part + 1) * hrows, :], wdt[s])

    for part in range(2):
        yacc[part * hrows:(part + 1) * hrows, :] = out_part(z, part)
    for step in range(steps):
        for part in range(2):
            s_up, got_up = hid_arrived(0, step, part)
            s_down, got_down = hid_arrived(1, step, part)
            got_up.wait()
            if step + 1 < steps or part == 0:
                hid(0, step + 1, part).start()
            got_down.wait()
            if step + 1 < steps or part == 1:
                hid(1, step + 1, part).start()
            yacc[part * hrows:(part + 1) * hrows, :] += out_part(s_up, part) + out_part(s_down, part)

    half_blocks = ne // 2
    place = y * nd + d
    for part in range(2):
        _, got = hid_arrived(part, steps, part)
        got.wait()
        total = yacc[part * hrows:(part + 1) * hrows, :] + out_part(far, part)
        ys[part * half_blocks:(part + 1) * half_blocks] = (
            total.reshape(half_blocks, cap, width).astype(BF16))

        def send_back(j, carry, part=part):
            dest = part * half_blocks + lax.rem(me + j * 11, half_blocks)

            @pl.when(dest != me)
            def _():
                pltpu.make_async_remote_copy(
                    src_ref=ys.at[dest], dst_ref=yb.at[place],
                    send_sem=y_send, recv_sem=y_recv,
                    device_id={"ep": dest}, device_id_type=MESH).start()
            return carry

        lax.fori_loop(0, half_blocks, send_back, 0)

    own = pltpu.make_async_copy(ys.at[me], yb.at[place], self_sem.at[1])
    own.start()
    own.wait()
    bytes_of(yb.at[pl.ds(0, ne - 1)], y_recv).wait()
    back = yb[...].reshape(rows, width)
    out_ref[...] = (dot(gate_high, back) + dot(gate_low, back)).astype(BF16)

    bytes_of(mb.at[pl.ds(0, nq - 1)], mk_send).wait()
    for r in range(count):
        bytes_of(tb.at[r, pl.ds(0, nq - 1)], tok_send.at[r]).wait()
        bytes_of(xs.at[r, pl.ds(0, nd - 1)], x_send.at[r]).wait()
    bytes_of(wdt.at[pl.ds(0, nh - 1)], wd_send).wait()
    bytes_of(ys.at[pl.ds(0, ne - 1)], y_send).wait()
    for direction in range(2):
        for part in range(nx):
            ring(direction, part).wait_send()
        for part in range(2):
            for step in range(steps):
                hid(direction, step, part).wait_send()
        hid(direction, steps, direction).wait_send()


def local(tokens, expert_ids, gate_scores, gate_weight, up_weight, down_weight):
    ne, nh, ny = lax.axis_size("ep"), lax.axis_size("hs"), CHIPS_Y
    count, model = tokens.shape
    width = model // nh
    part_width = width // CORES
    units = gate_weight.shape[2]
    cap = max(2, 2 * expert_ids.shape[1] * count // ne)
    rows = ne * cap
    nq, nd, nx = ny * CORES, ne // ny, ne // (ny * CORES)
    slices = (0,) + tuple(range(2, nh - 1))
    rounds = len(slices)
    steps = nh // 2 - 1
    dma = pltpu.SemaphoreType.DMA
    hbm = pl.BlockSpec(memory_space=pltpu.MemorySpace.HBM)
    vmem = pl.BlockSpec(memory_space=pltpu.MemorySpace.VMEM)
    return pl.pallas_call(
        functools.partial(kernel, ne, nh, ny, cap, slices),
        out_shape=jax.ShapeDtypeStruct((count, width), BF16),
        in_specs=[hbm, vmem, vmem, hbm, hbm, hbm],
        out_specs=vmem,
        scratch_shapes=[
            pltpu.VMEM((count, model), BF16),
            pltpu.VMEM((ny, nd, 128), F32),
            pltpu.VMEM((nq, nd, 128), F32),
            pltpu.VMEM((rounds, nq, count, part_width), BF16),
            pltpu.VMEM((nd, nq * cap, nq * count), BF16),
            pltpu.VMEM((rounds, nd, nq * cap, part_width), BF16),
            pltpu.VMEM((nh, nx, nq * cap, width), BF16),
            pltpu.VMEM((model, 2 * units), BF16),
            pltpu.VMEM((nh, units, width), BF16),
            pltpu.VMEM((rows, 2 * units), F32),
            pltpu.VMEM((nh, rows, units), BF16),
            pltpu.VMEM((ne, cap, width), BF16),
            pltpu.VMEM((ne, cap, width), BF16),
            pltpu.VMEM((rows, width), F32),
            dma((4,)), dma((rounds,)), dma((2,)), dma, dma, dma((rounds,)), dma((rounds,)),
            dma((rounds,)), dma((rounds,)), dma, dma,
            dma((2, nx)), dma((2, nx)),
            dma((2, steps + 1, 2)), dma((2, steps + 1, 2)), dma, dma,
        ],
        compiler_params=pltpu.CompilerParams(
            collective_id=0, has_side_effects=True, vmem_limit_bytes=63 << 20),
    )(tokens, expert_ids.T, gate_scores.T, gate_weight, up_weight, down_weight)


def solution(mesh):
    placed = (
        P("ep", None),
        P("ep", None),
        P("ep", None),
        P("ep", None, "hs"),
        P("ep", None, "hs"),
        P("ep", "hs", None),
    )
    return jax.shard_map(
        local, mesh=mesh, in_specs=placed, out_specs=P("ep", "hs"), check_vma=False
    )
```

time: 108 us -> 95 us (0.88)
  the two profiles are of different devices: /device:TPU:1 before, /device:TPU:5 now
where the time goes in v2:
time: 95 us; the launch traced here: 94.8 us
  Pallas kernels  93.4 us (98%)
  local copies, waits for them, and re-layouts  1.38 us (1%)
    pallas_call x1, Pallas kernels, local(): pl.pallas_call(functools.partial(kernel, ne, nh, ny, cap, slices), out_sh...  93.4 us

profile of v2, /device:TPU:5, one launch (start us, length us, event | category | flops | bytes accessed | tf_op | source)
XLA Modules:
  0.0 94.8 jit_solution(16323567857303085823)
XLA Ops:
  0.0 93.4 %shard_map.64 = bf16[32,512]{1,0:T(8,128)(2,1)} custom-call(bf16[32,4096]{1,0:T(8,128)(2,1)} %tok_hbm.1, s32[8,32]{1,0:T(8,128)} %bitcast.2, f32[8,32]{1,0:T(8,128)} %bitcast.3, bf16[1,4096,128]{2,1,0:T(8,128)(2,1)} %wg_hbm.1, bf16[1,4096,128]{2,1,0:T(8,128)(2,1)} %wu_hbm.1, bf16[1,128,4096]{2,1,0:T(8,128)(2,1)} %wd_hbm.1), custom_call_target="tpu_custom_call" | custom-call | tf_op jit(solution)/shard_map/pallas_call | solution.py:333
  93.4 1.4 %copy.8 = bf16[32,512]{1,0:T(8,128)(2,1)} copy(bf16[32,512]{1,0:T(8,128)(2,1)} %shard_map.64) | data formatting | bytes 65536

commit v3 on v2

--- a/solution.py
+++ b/solution.py
@@ -28,7 +28,7 @@
     return jnp.where(condition, 1.0, 0.0).astype(BF16)
 
 
-def kernel(ne, nh, ny, cap, slices,
+def kernel(ne, nh, ny, cap, slices, late,
            tok_hbm, ids_ref, score_ref, wg_hbm, wu_hbm, wd_hbm, out_ref,
            tok_v, mk, mb, tb, pick, xs, xb, wgu, wdt, acc, hb, ys, yb, yacc,
            load_sem, own_sem, self_sem, mk_send, mk_recv, tok_send, tok_recv, x_send, x_recv,
@@ -51,6 +51,8 @@
     q = lax.rem(me, nq)
     d = x * nc + c
     count = len(slices)
+    offsets = (0,) + tuple(o for i in range(1, nx // 2) for o in (i, nx - i)) + (nx // 2,)
+    chunks = [lax.rem(x + offset, nx) for offset in offsets]
     up_z, down_z = lax.rem(z + 1, nh), lax.rem(z + nh - 1, nh)
     far = lax.rem(z + half, nh)
 
@@ -69,6 +71,10 @@
 
     lax.fori_loop(1, ne, greet_ep, 0)
     lax.fori_loop(1, nh, greet_hs, 0)
+
+    def routed(r, core):
+        base, by_core = slices[r]
+        return plane(base + by_core * core)
 
     def columns(s):
         return pl.ds(pl.multiple_of(s * width, width), width)
@@ -83,8 +89,8 @@
         pltpu.make_async_copy(wd_hbm.at[0, :, columns(z)], wdt.at[z], load_sem.at[3]),
     ]
     own_tokens = [
-        pltpu.make_async_copy(tok_hbm.at[:, part_columns(plane(rel), c)], tb.at[r, q], own_sem.at[r])
-        for r, rel in enumerate(slices)
+        pltpu.make_async_copy(tok_hbm.at[:, part_columns(routed(r, c), c)], tb.at[r, q], own_sem.at[r])
+        for r in range(count)
     ]
     for load in loads[:1] + own_tokens + loads[1:]:
         load.start()
@@ -110,14 +116,15 @@
     pl.semaphore_wait(barrier, ne - 1 + nh - 1)
 
     def along_y(j):
-        other = lax.rem(q + j, nq)
+        other = lax.rem(q + j * 5, nq)
         return other, {"ep": x * nq + other}
 
-    def send_tokens(r, rel):
+    def send_tokens(r):
         def body(j, carry):
             other, device = along_y(j)
             pltpu.make_async_remote_copy(
-                src_ref=tok_v.at[:, part_columns(plane(rel), lax.rem(other, nc))], dst_ref=tb.at[r, q],
+                src_ref=tok_v.at[:, part_columns(routed(r, lax.rem(other, nc)), lax.rem(other, nc))],
+                dst_ref=tb.at[r, q],
                 send_sem=tok_send.at[r], recv_sem=tok_recv.at[r],
                 device_id=device, device_id_type=MESH).start()
             return carry
@@ -133,7 +140,7 @@
     lax.fori_loop(1, nq, send_marks, 0)
     own_marks = pltpu.make_async_copy(mk.at[y], mb.at[q], self_sem.at[0])
     own_marks.start()
-    send_tokens(0, slices[0])
+    send_tokens(0)
 
     def send_down(j, carry):
         dest = lax.rem(z + j, nh)
@@ -143,9 +150,11 @@
             device_id={"hs": dest}, device_id_type=MESH).start()
         return carry
 
-    lax.fori_loop(1, nh, send_down, 0)
+    lax.fori_loop(half - 1, half + 2, send_down, 0)
+    lax.fori_loop(1, half - 1, send_down, 0)
+    lax.fori_loop(half + 2, nh, send_down, 0)
     for r in range(1, count):
-        send_tokens(r, slices[r])
+        send_tokens(r)
 
     spread = ones_where(iota((rows, ne), 0) // cap == iota((rows, ne), 1))
     here = dot(spread, mark) == (lax.rem(iota((rows, tokens), 0), cap) + 1).astype(F32)
@@ -172,126 +181,163 @@
         own_tokens[r].wait()
         bytes_of(tb.at[r, pl.ds(0, nq - 1)], tok_recv.at[r]).wait()
         block = tb[r].reshape(q_lanes, part_width)
-        s = plane(slices[r])
-
-        def body(j, carry):
-            i = lax.rem(d + j, nd)
+        s = routed(r, c)
+
+        def send_selected(i):
             xs[r, i] = dot(pick[i], block).astype(BF16)
             pltpu.make_async_remote_copy(
                 src_ref=xs.at[r, i],
                 dst_ref=xb.at[s, x, :, pl.ds(pl.multiple_of(c * part_width, part_width), part_width)],
-                send_sem=x_send.at[r], recv_sem=x_recv.at[r],
+                send_sem=x_send.at[r], recv_sem=x_recv.at[r, lax.rem(x - i // nc + nx, nx)],
                 device_id={"ep": (i // nc * ny + y) * nc + lax.rem(i, nc)}, device_id_type=MESH).start()
-            return carry
-
-        lax.fori_loop(1, nd, body, 0)
+
+        send_selected(x * nc + lax.rem(c + 1, nc))
         xb[s, x, :, pl.ds(pl.multiple_of(c * part_width, part_width), part_width)] = (
             dot(pick[d], block).astype(BF16))
+        for offset in offsets[1:]:
+            def body(j, carry, offset=offset):
+                send_selected(lax.rem(x + offset, nx) * nc + j)
+                return carry
+            lax.fori_loop(0, nc, body, 0)
+
+    def selected(r, offset):
+        bytes_of(xs.at[r, pl.ds(0, nc if offset else nc - 1)], x_recv.at[r, offset]).wait()
 
     def weights(s):
         return wgu[pl.ds(pl.multiple_of(s * width, width), width), :]
 
     def multiply(s, first=False):
-        product = dot(xb[s].reshape(rows, width), weights(s))
+        product = dot(xb[s].reshape(rows, width), weights(s)).reshape(acc.shape)
         if first:
             acc[...] = product
         else:
             acc[...] += product
 
-    def ring(direction, part):
-        view = xb.at[z, part]
+    def ring_view(s, step, direction, k):
+        if step == 0:
+            return xb.at[s, chunks[k]]
+        return xb.at[s, chunks[k], :, pl.ds(direction * part_width, part_width)]
+
+    def ring(direction, step, k):
+        view = ring_view(plane(-step) if direction == 0 else plane(step), step, direction, k)
         return pltpu.make_async_remote_copy(
             src_ref=view, dst_ref=view,
-            send_sem=ring_send.at[direction, part], recv_sem=ring_recv.at[direction, part],
+            send_sem=ring_send.at[direction, step, k], recv_sem=ring_recv.at[direction, step, k],
             device_id={"hs": up_z if direction == 0 else down_z}, device_id_type=MESH)
 
+    def ring_arrived(direction, step, k):
+        s = plane(-1 - step) if direction == 0 else plane(1 + step)
+        return bytes_of(ring_view(s, step, direction, k), ring_recv.at[direction, step, k])
+
     def collect(r):
-        bytes_of(xs.at[r, pl.ds(0, nd - 1)], x_recv.at[r]).wait()
+        for offset in offsets:
+            selected(r, offset)
         if r == 0:
-            for part in range(nx):
-                ring(0, part).start()
-                ring(1, part).start()
+            for k in range(nx):
+                ring(0, 0, k).start()
+                ring(1, 0, k).start()
             loads[1].wait()
             loads[2].wait()
-        multiply(plane(slices[r]), first=r == 0)
+        if slices[r][1] == 0:
+            multiply(plane(slices[r][0]), first=r == 0)
 
     select(0)
     for r in range(1, count):
         select(r)
-        collect(r - 1)
-
-    for direction, s in ((0, plane(-1)), (1, plane(1))):
-        for part in range(nx):
-            view = xb.at[s, part]
-            bytes_of(view, ring_recv.at[direction, part]).wait()
-        multiply(s)
-    collect(count - 1)
+        if r < count - late + 1:
+            collect(r - 1)
+
+    for k in range(nx):
+        for direction in range(2):
+            ring_arrived(direction, 0, k).wait()
+            ring(direction, 1, k).start()
+    multiply(plane(-1))
+    multiply(plane(1))
 
     steps = half - 1
-    hrows = rows // 2
-
-    def hid(direction, step, part):
+
+    def antipode(k):
+        return 0 if k < nx // 2 else 1
+
+    def hid(direction, step, k):
         s = plane(-step) if direction == 0 else plane(step)
-        view = hb.at[s, pl.ds(part * hrows, hrows)]
+        view = hb.at[s, chunks[k]]
         return pltpu.make_async_remote_copy(
             src_ref=view, dst_ref=view,
-            send_sem=hid_send.at[direction, step, part], recv_sem=hid_recv.at[direction, step, part],
+            send_sem=hid_send.at[direction, step, k], recv_sem=hid_recv.at[direction, step, k],
             device_id={"hs": up_z if direction == 0 else down_z}, device_id_type=MESH)
 
-    def hid_arrived(direction, step, part):
+    def hid_arrived(direction, step, k):
         s = plane(-1 - step) if direction == 0 else plane(1 + step)
-        view = hb.at[s, pl.ds(part * hrows, hrows)]
-        return s, bytes_of(view, hid_recv.at[direction, step, part])
-
-    for part in range(2):
-        gate = acc[part * hrows:(part + 1) * hrows, 0:units]
-        upper = acc[part * hrows:(part + 1) * hrows, units:2 * units]
-        hb[z, part * hrows:(part + 1) * hrows, :] = (
-            gate / (1.0 + jnp.exp(-gate)) * upper).astype(BF16)
-        hid(0, 0, part).start()
-        hid(1, 0, part).start()
-
+        return s, bytes_of(hb.at[s, chunks[k]], hid_recv.at[direction, step, k])
+
+    def out_part(s, k):
+        return dot(hb[s, chunks[k]], wdt[s])
+
+    def make_hidden(k):
+        total = acc[chunks[k]]
+        for direction, s in ((0, plane(-2)), (1, plane(2))):
+            ring_arrived(direction, 1, k).wait()
+            total = total + dot(xb[s, chunks[k]], weights(s))
+        for r in range(count - late, count):
+            selected(r, offsets[k])
+            s = plane(slices[r][0])
+            total = total + dot(xb[s, chunks[k]], weights(s))
+        gate, upper = total[:, 0:units], total[:, units:2 * units]
+        hb[z, chunks[k]] = (gate / (1.0 + jnp.exp(-gate)) * upper).astype(BF16)
+        hid(0, 0, k).start()
+        hid(1, 0, k).start()
+
+    def pass_hidden(k, step):
+        s_up, got_up = hid_arrived(0, step, k)
+        s_down, got_down = hid_arrived(1, step, k)
+        got_up.wait()
+        if step + 1 < steps or antipode(k) == 0:
+            hid(0, step + 1, k).start()
+        got_down.wait()
+        if step + 1 < steps or antipode(k) == 1:
+            hid(1, step + 1, k).start()
+        if step == 0:
+            yacc[chunks[k]] = out_part(z, k) + out_part(s_up, k) + out_part(s_down, k)
+        else:
+            yacc[chunks[k]] += out_part(s_up, k) + out_part(s_down, k)
+
+    place = y * nd + d
+
+    def finish(k):
+        _, got = hid_arrived(antipode(k), steps, k)
+        got.wait()
+        total = yacc[chunks[k]] + out_part(far, k)
+        ys[pl.ds(chunks[k] * nq, nq)] = total.reshape(nq, cap, width).astype(BF16)
+
+        def send_back(j, carry):
+            dest = chunks[k] * nq + lax.rem(q + j * 5, nq)
+            pltpu.make_async_remote_copy(
+                src_ref=ys.at[dest], dst_ref=yb.at[place],
+                send_sem=y_send, recv_sem=y_recv,
+                device_id={"ep": dest}, device_id_type=MESH).start()
+            return carry
+
+        lax.fori_loop(1 if k == 0 else 0, nq, send_back, 0)
+
+    make_hidden(0)
     loads[3].wait()
-    bytes_of(wdt.at[pl.ds(0, nh - 1)], wd_recv).wait()
-
-    def out_part(s, part):
-        return dot(hb[s, part * hrows:(part + 1) * hrows, :], wdt[s])
-
-    for part in range(2):
-        yacc[part * hrows:(part + 1) * hrows, :] = out_part(z, part)
-    for step in range(steps):
-        for part in range(2):
-            s_up, got_up = hid_arrived(0, step, part)
-            s_down, got_down = hid_arrived(1, step, part)
-            got_up.wait()
-            if step + 1 < steps or part == 0:
-                hid(0, step + 1, part).start()
-            got_down.wait()
-            if step + 1 < steps or part == 1:
-                hid(1, step + 1, part).start()
-            yacc[part * hrows:(part + 1) * hrows, :] += out_part(s_up, part) + out_part(s_down, part)
-
-    half_blocks = ne // 2
-    place = y * nd + d
-    for part in range(2):
-        _, got = hid_arrived(part, steps, part)
-        got.wait()
-        total = yacc[part * hrows:(part + 1) * hrows, :] + out_part(far, part)
-        ys[part * half_blocks:(part + 1) * half_blocks] = (
-            total.reshape(half_blocks, cap, width).astype(BF16))
-
-        def send_back(j, carry, part=part):
-            dest = part * half_blocks + lax.rem(me + j * 11, half_blocks)
-
-            @pl.when(dest != me)
-            def _():
-                pltpu.make_async_remote_copy(
-                    src_ref=ys.at[dest], dst_ref=yb.at[place],
-                    send_sem=y_send, recv_sem=y_recv,
-                    device_id={"ep": dest}, device_id_type=MESH).start()
-            return carry
-
-        lax.fori_loop(0, half_blocks, send_back, 0)
+    for k in range(1, nx):
+        make_hidden(k)
+        if k == 1:
+            bytes_of(wdt.at[pl.ds(0, nh - 1)], wd_recv).wait()
+        if k <= steps:
+            pass_hidden(0, k - 1)
+    for step in range(nx - 1, steps):
+        pass_hidden(0, step)
+    for k in range(1, nx):
+        pass_hidden(k, 0)
+    finish(0)
+    for step in range(1, steps):
+        for k in range(1, nx):
+            pass_hidden(k, step)
+    for k in range(1, nx):
+        finish(k)
 
     own = pltpu.make_async_copy(ys.at[me], yb.at[place], self_sem.at[1])
     own.start()
@@ -307,12 +353,12 @@
     bytes_of(wdt.at[pl.ds(0, nh - 1)], wd_send).wait()
     bytes_of(ys.at[pl.ds(0, ne - 1)], y_send).wait()
     for direction in range(2):
-        for part in range(nx):
-            ring(direction, part).wait_send()
-        for part in range(2):
-            for step in range(steps):
-                hid(direction, step, part).wait_send()
-        hid(direction, steps, direction).wait_send()
+        for k in range(nx):
+            for step in range(2):
+                ring(direction, step, k).wait_send()
+        for k in range(nx):
+            for step in range(steps + (1 if antipode(k) == direction else 0)):
+                hid(direction, step, k).wait_send()
 
 
 def local(tokens, expert_ids, gate_scores, gate_weight, up_weight, down_weight):
@@ -324,14 +370,14 @@
     cap = max(2, 2 * expert_ids.shape[1] * count // ne)
     rows = ne * cap
     nq, nd, nx = ny * CORES, ne // ny, ne // (ny * CORES)
-    slices = (0,) + tuple(range(2, nh - 1))
+    slices = ((0, 0), (2, -4)) + tuple((i, 0) for i in range(3, nh - 2))
     rounds = len(slices)
     steps = nh // 2 - 1
     dma = pltpu.SemaphoreType.DMA
     hbm = pl.BlockSpec(memory_space=pltpu.MemorySpace.HBM)
     vmem = pl.BlockSpec(memory_space=pltpu.MemorySpace.VMEM)
     return pl.pallas_call(
-        functools.partial(kernel, ne, nh, ny, cap, slices),
+        functools.partial(kernel, ne, nh, ny, cap, slices, min(2, rounds - 2)),
         out_shape=jax.ShapeDtypeStruct((count, width), BF16),
         in_specs=[hbm, vmem, vmem, hbm, hbm, hbm],
         out_specs=vmem,
@@ -345,15 +391,15 @@
             pltpu.VMEM((nh, nx, nq * cap, width), BF16),
             pltpu.VMEM((model, 2 * units), BF16),
             pltpu.VMEM((nh, units, width), BF16),
-            pltpu.VMEM((rows, 2 * units), F32),
-            pltpu.VMEM((nh, rows, units), BF16),
+            pltpu.VMEM((nx, nq * cap, 2 * units), F32),
+            pltpu.VMEM((nh, nx, nq * cap, units), BF16),
             pltpu.VMEM((ne, cap, width), BF16),
             pltpu.VMEM((ne, cap, width), BF16),
-            pltpu.VMEM((rows, width), F32),
+            pltpu.VMEM((nx, nq * cap, width), F32),
             dma((4,)), dma((rounds,)), dma((2,)), dma, dma, dma((rounds,)), dma((rounds,)),
-            dma((rounds,)), dma((rounds,)), dma, dma,
-            dma((2, nx)), dma((2, nx)),
-            dma((2, steps + 1, 2)), dma((2, steps + 1, 2)), dma, dma,
+            dma((rounds,)), dma((rounds, nx)), dma, dma,
+            dma((2, 2, nx)), dma((2, 2, nx)),
+            dma((2, steps + 1, nx)), dma((2, steps + 1, nx)), dma, dma,
         ],
         compiler_params=pltpu.CompilerParams(
             collective_id=0, has_side_effects=True, vmem_limit_bytes=63 << 20),

time: 95 us -> 89.7 us (0.944)
  the two profiles are of different devices: /device:TPU:5 before, /device:TPU:1 now
where the time goes in v3:
time: 89.7 us; the launch traced here: 89.5 us
  Pallas kernels  88.1 us (98%)
  local copies, waits for them, and re-layouts  1.38 us (2%)
    pallas_call x1, Pallas kernels, local(): pl.pallas_call(functools.partial(kernel, ne, nh, ny, cap, slices, min(2,...  88.1 us

profile of v3, /device:TPU:1, one launch (start us, length us, event | category | flops | bytes accessed | tf_op | source)
XLA Modules:
  0.0 89.5 jit_solution(5378279102004926072)
XLA Ops:
  0.0 88.1 %shard_map.64 = bf16[32,512]{1,0:T(8,128)(2,1)} custom-call(bf16[32,4096]{1,0:T(8,128)(2,1)} %tok_hbm.1, s32[8,32]{1,0:T(8,128)} %bitcast.2, f32[8,32]{1,0:T(8,128)} %bitcast.3, bf16[1,4096,128]{2,1,0:T(8,128)(2,1)} %wg_hbm.1, bf16[1,4096,128]{2,1,0:T(8,128)(2,1)} %wu_hbm.1, bf16[1,128,4096]{2,1,0:T(8,128)(2,1)} %wd_hbm.1), custom_call_target="tpu_custom_call" | custom-call | tf_op jit(solution)/shard_map/pallas_call | solution.py:379
  88.1 1.4 %copy.8 = bf16[32,512]{1,0:T(8,128)(2,1)} copy(bf16[32,512]{1,0:T(8,128)(2,1)} %shard_map.64) | data formatting | bytes 65536
